TPU v7x, 32 devices: a whole 2x2x4 slice. The times are simulated.
32 devices in a mesh: rep: 4 (over z), shard: 8 (over y, x, core).
Axes of the slice: x: 2, y: 2, z: 4, core: 2. Of those that a mesh axis runs over, the one named last changes fastest.
Arguments:
- tokens: bfloat16 [8192, 1024], P(('rep', 'shard')), may hold values from -6 to 6
- prefix: int32 [32], P(('rep', 'shard')), may hold values from 25 to 128
- routes: int32 [8192, 8], P(('rep', 'shard')), may hold values from 0 to 31, all different within a row; in each aligned block of 256 rows (0 to 255, 256 to 511, ...) at most 96 rows name the same one
- cotangent: bfloat16 [8192, 1024], P(('rep', 'shard')), may hold values from -6 to 6
- w_query: bfloat16 [1024, 1024], P('shard'), may hold values from -0.625 to 0.625
- key_weight: bfloat16 [1024, 512], P('shard'), may hold values from -0.625 to 0.625
- value_weight: bfloat16 [1024, 512], P('shard'), may hold values from -0.1875 to 0.1875
- w_out: bfloat16 [1024, 1024], P('shard'), may hold values from -6 to 6
- norm_attn: bfloat16 [1024], P('shard'), may hold values from 0.5 to 1.5
- norm_moe: bfloat16 [1024], P('shard'), may hold values from 0.5 to 1.5
- w_router: bfloat16 [1024, 32], P('shard'), may hold values from -0.09375 to 0.09375
- w_gate: bfloat16 [32, 1024, 512], P('shard'), may hold values from -0.1875 to 0.1875
- w_up: bfloat16 [32, 1024, 512], P('shard'), may hold values from -0.1875 to 0.1875
- w_down: bfloat16 [32, 512, 1024], P('shard'), may hold values from -6 to 6
Outputs:
- layer_out: bfloat16 [8192, 1024], P(('rep', 'shard'))
- d_tokens: float32 [8192, 1024], P(('rep', 'shard'))
- d_w_query: float32 [1024, 1024], P('shard')
- d_w_key: float32 [1024, 512], P('shard')
- d_w_value: float32 [1024, 512], P('shard')
- d_w_out: float32 [1024, 1024], P('shard')
- d_norm_attn: float32 [1024], P('shard')
- d_norm_moe: float32 [1024], P('shard')
- d_w_router: float32 [1024, 32], P('shard')
- d_w_gate: float32 [32, 1024, 512], P('shard')
- d_w_up: float32 [32, 1024, 512], P('shard')
- d_w_down: float32 [32, 512, 1024], P('shard')
Inputs may be any that keep to these rules, and one draw needn't show every extreme that they name: `routes`: each row names 8 different experts; among the rows of one device no expert is named more than 96 times, and in every draw some device's rows name some expert exactly 96 times.
All inputs are finite; a program needn't handle non-finite values.
Results may differ from a plain program's by a relative error of at most 0.024.
Values may be sent and summed in bfloat16 or wider, within the bound.
A program may use at most 256 MiB of HBM per device.

v0:
```python
import functools
import math

import jax
import jax.numpy as jnp
import numpy as np
from jax import lax
from jax.experimental import pallas as pl
from jax.experimental.pallas import tpu as pltpu
from jax.sharding import PartitionSpec as P

QUERY_HEADS = 16
KEY_VALUE_HEADS = 8
HEAD_SIZE = 64
CAP = 96
LANES = 128
GATHERED_REPLICAS = 4

epsilon = 1e-06
score_scale = 0.015625
branch_scale = 0.22
masked_value = -1e30

f32 = jnp.float32
bf16 = jnp.bfloat16
MESH = pl.DeviceIdType.MESH


def dot(left, right, contract=((1,), (0,))):
    return lax.dot_general(left, right, (contract, ((), ())), preferred_element_type=f32)

def slot_ranks(gates):
    tokens = gates.shape[1]
    named = gates > 0
    before = lax.broadcasted_iota(jnp.int32, (tokens, tokens), 0) < lax.broadcasted_iota(jnp.int32, (tokens, tokens), 1)
    rank = dot(named.astype(f32).astype(bf16), before.astype(f32).astype(bf16))
    return jnp.where(named, rank, -1.0)

def pick_row(table, row):
    here = lax.broadcasted_iota(jnp.int32, table.shape, 0) == row
    return jnp.sum(jnp.where(here, table, 0.0), axis=0, keepdims=True)

def slot_one_hot(ranks, first, local):
    tokens = ranks.shape[1]
    slot = lax.broadcasted_iota(jnp.int32, (CAP, tokens), 0).astype(f32)
    return [jnp.where(pick_row(ranks, first + l) == slot, 1.0, 0.0) for l in range(local)]

def gather_block(x, c, gates, first, local, xg_ref, cg_ref, sg_ref, at):
    ranks = slot_ranks(gates)
    parts = slot_one_hot(ranks, first, local)
    table = jnp.concatenate(parts, axis=0).astype(bf16)
    xg = dot(table, x).astype(bf16)
    cg = dot(table, c).astype(bf16)
    for l in range(local):
        rows = slice(l * CAP, (l + 1) * CAP)
        xg_ref[l, pl.ds(at, CAP), :] = xg[rows]
        cg_ref[l, pl.ds(at, CAP), :] = cg[rows]
        gate = jnp.sum(parts[l] * pick_row(gates, first + l), axis=1, keepdims=True)
        sg_ref[l, pl.ds(at, CAP), :] = branch_scale * gate
    return parts

def expert_parts(xg, cg, scale, wg, wu, wd):
    gate_part = dot(xg, wg)
    up_part = dot(xg, wu)
    raw = dot(cg, wd, ((1,), (1,)))
    sigma = 1.0 / (1.0 + jnp.exp(-gate_part))
    act = gate_part * sigma
    inner = act * up_part
    d_inner = raw * scale
    d_gate = (d_inner * up_part * (sigma + act * (1.0 - sigma))).astype(bf16)
    d_up = (d_inner * act).astype(bf16)
    scaled = (inner * scale).astype(bf16)
    return inner, raw, d_gate, d_up, scaled

def add_expert(l, xg_ref, cg_ref, sg_ref, wg, wu, wd, ag, au, ad):
    xg, cg = xg_ref[l], cg_ref[l]
    _, _, d_gate, d_up, scaled = expert_parts(xg, cg, sg_ref[l], wg[l], wu[l], wd[l])
    ag[l] += dot(xg, d_gate, ((0,), (0,)))
    au[l] += dot(xg, d_up, ((0,), (0,)))
    ad[l] += dot(scaled, cg, ((0,), (0,)))

def late_places(rep, reps):
    later = (rep + reps - 1) // reps
    return later * (reps - 2), (1 - later) * (reps - 2)

def sums_kernel(nb, more, x_hbm, c_hbm, g_ref, wg_hbm, wu_hbm, wd_hbm, *rest):
    if len(x_hbm.shape) == 4:
        _, left = late_places(lax.axis_index("rep"), lax.axis_size("rep"))
        x_hbm, c_hbm = x_hbm.at[left], c_hbm.at[left]
    starts, (og_hbm, ou_hbm, od_hbm, *scratch) = rest[:3 * more], rest[3 * more:]
    sums_body(nb, starts, x_hbm, c_hbm, g_ref, wg_hbm, wu_hbm, wd_hbm, og_hbm, ou_hbm, od_hbm, *scratch)

def sums_body(nb, starts, x_hbm, c_hbm, g_ref, wg_hbm, wu_hbm, wd_hbm, og_hbm, ou_hbm, od_hbm,
                xbuf, cbuf, wg, wu, wd, ag, au, ad, xg_ref, cg_ref, sg_ref, sem, wsem, asem):
    local = wg.shape[0]
    blocks = x_hbm.shape[0]
    chunks = blocks // nb
    first = lax.axis_index("shard") * local
    def fetch(i, slot):
        return (pltpu.make_async_copy(x_hbm.at[pl.ds(i * nb, nb)], xbuf.at[slot], sem.at[0, slot]),
                pltpu.make_async_copy(c_hbm.at[pl.ds(i * nb, nb)], cbuf.at[slot], sem.at[1, slot]))
    for cp in fetch(0, 0):
        cp.start()
    weights = [pltpu.make_async_copy(a, b, wsem.at[i]) for i, (a, b) in enumerate(((wg_hbm, wg), (wu_hbm, wu), (wd_hbm, wd)))]
    for cp in weights:
        cp.start()
    loads = [
        pltpu.make_async_copy(a.at[l], b.at[l], asem.at[i, l])
        for l in range(local) for i, (a, b) in enumerate(zip(starts, (ag, au, ad)))
    ]
    for cp in loads:
        cp.start()
    if not starts:
        ag[...] = jnp.zeros_like(ag)
        au[...] = jnp.zeros_like(au)
        ad[...] = jnp.zeros_like(ad)
    for cp in weights:
        cp.wait()

    def chunk(i, carry):
        slot = lax.rem(i, 2)
        @pl.when(i + 1 < chunks)
        def _():
            for cp in fetch(i + 1, 1 - slot):
                cp.start()
        for cp in fetch(i, slot):
            cp.wait()
        def block(b, carry):
            gather_block(xbuf[slot, b], cbuf[slot, b], g_ref[i * nb + b], first, local, xg_ref, cg_ref, sg_ref,
                         pl.multiple_of(b * CAP, CAP))
            return carry
        lax.fori_loop(0, nb, block, 0)
        def expert(l, carry):
            if starts:
                @pl.when(i == 0)
                def _():
                    for k, (a, b) in enumerate(zip(starts, (ag, au, ad))):
                        pltpu.make_async_copy(a.at[l], b.at[l], asem.at[k, l]).wait()
            add_expert(l, xg_ref, cg_ref, sg_ref, wg, wu, wd, ag, au, ad)

            @pl.when(i == chunks - 1)
            def _():
                for k, (a, b) in enumerate(((ag, og_hbm), (au, ou_hbm), (ad, od_hbm))):
                    pltpu.make_async_copy(a.at[l], b.at[l], asem.at[k, l]).start()
            return carry
        lax.fori_loop(0, local, expert, 0)
        return carry
    lax.fori_loop(0, chunks, chunk, 0)
    for l in range(local):
        for k, (a, b) in enumerate(((ag, og_hbm), (au, ou_hbm), (ad, od_hbm))):
            pltpu.make_async_copy(a.at[l], b.at[l], asem.at[k, l]).wait()

def moe_sums(x, c, gates, wg, wu, wd, starts=(), nb=4):
    blocks, tokens, width = x.shape[-3:]
    local, _, hidden = wg.shape
    any_ = pl.BlockSpec(memory_space=pl.ANY)
    rows = nb * CAP
    return pl.pallas_call(
        functools.partial(sums_kernel, nb, bool(starts)),
        out_shape=[jax.ShapeDtypeStruct(w.shape, f32) for w in (wg, wu, wd)],
        in_specs=[any_, any_, pl.BlockSpec(memory_space=pltpu.VMEM), any_, any_, any_] + [any_] * len(starts),
        out_specs=[any_] * 3,
        scratch_shapes=[
            pltpu.VMEM((2, nb, tokens, width), bf16), pltpu.VMEM((2, nb, tokens, width), bf16),
            pltpu.VMEM(wg.shape, bf16), pltpu.VMEM(wu.shape, bf16), pltpu.VMEM(wd.shape, bf16),
            pltpu.VMEM(wg.shape, f32), pltpu.VMEM(wu.shape, f32), pltpu.VMEM(wd.shape, f32),
            pltpu.VMEM((local, rows, width), bf16), pltpu.VMEM((local, rows, width), bf16), pltpu.VMEM((local, rows, 1), f32),
            pltpu.SemaphoreType.DMA((2, 2)), pltpu.SemaphoreType.DMA((3,)), pltpu.SemaphoreType.DMA((3, local)),
        ],
        compiler_params=pltpu.CompilerParams(vmem_limit_bytes=60 << 20),
        cost_estimate=pl.CostEstimate(
            flops=12 * blocks * local * CAP * width * hidden, transcendentals=blocks * local * CAP * hidden,
            bytes_accessed=4 * blocks * tokens * width + 24 * wg.size,
        ),
        name="expert_sums",
    )(x, c, gates, wg, wu, wd, *starts)


def norm_scale(rows):
    return lax.rsqrt(jnp.mean(rows * rows, axis=-1, keepdims=True) + epsilon)

def flip(index, bit):
    return index + bit - 2 * bit * ((index // bit) % 2)

def turned(index, core, step, bits):
    return (1 - core) * flip(index, bits[step]) + core * flip(index, bits[-1 - step])

def greet(spread):
    rep, me = lax.axis_index("rep"), lax.axis_index("shard")
    shards, reps = lax.axis_size("shard"), lax.axis_size("rep")
    peers = [(rep, (me + j) % shards) for j in range(1, shards)]
    if spread:
        peers += [((rep + j) % reps, me) for j in range(1, reps)]
    barrier = pltpu.get_barrier_semaphore()
    for peer in peers:
        pl.semaphore_signal(barrier, inc=1, device_id=peer, device_id_type=MESH)
    pl.semaphore_wait(barrier, len(peers))


class PlaneGather:
    def __init__(self, buf, own, send, recv, base=0):
        self.buf, self.own, self.send, self.recv, self.base = buf, own, send, recv, base
        self.rep, self.me = lax.axis_index("rep"), lax.axis_index("shard")
        self.core = self.me % 2
        shards = lax.axis_size("shard")
        self.bits = [1 << i for i in range(1, shards.bit_length() - 1)]
        self.steps = len(self.bits)

    @staticmethod
    def copies(shards):
        return (shards // 2 - 1) + shards // 2

    def owner(self, of, subset):
        for step in range(self.steps):
            if subset >> step & 1:
                of = turned(of, self.core, step, self.bits)
        return of

    def copy(self, number, subset, target):
        owner = self.owner(self.me, subset)
        return pltpu.make_async_remote_copy(
            src_ref=self.buf.at[owner] if subset else self.own, dst_ref=self.buf.at[owner],
            send_sem=self.send.at[self.base + number], recv_sem=self.recv.at[self.base + number],
            device_id=(self.rep, target), device_id_type=MESH,
        )

    def chip_copy(self, step, subset):
        return self.copy((1 << step) - 1 + subset, subset, turned(self.me, self.core, step, self.bits))

    def core_copy(self, subset):
        return self.copy((1 << self.steps) - 1 + subset, subset, flip(self.me, 1))

    def start(self):
        for step in range(self.steps):
            self.chip_copy(step, 0).start()
        self.core_copy(0).start()

    def forward(self, step):
        for subset in range(1 << step):
            self.chip_copy(step, subset).wait_recv()
            whole = subset + (1 << step)
            for later in range(step + 1, self.steps):
                self.chip_copy(later, whole).start()
            self.core_copy(whole).start()

    def finish(self):
        for subset in range(1 << self.steps):
            self.core_copy(subset).wait_recv()
        self.sent()

    def sent(self):
        for step in range(self.steps):
            for subset in range(1 << step):
                self.chip_copy(step, subset).wait_send()
        for subset in range(1 << self.steps):
            self.core_copy(subset).wait_send()

class RepSends:
    def __init__(self, buf, own, send, recv, neighbours):
        rep, me, reps = lax.axis_index("rep"), lax.axis_index("shard"), lax.axis_size("rep")
        self.rep, self.reps, self.neighbours = rep, reps, neighbours
        self.copies = [
            pltpu.make_async_remote_copy(
                src_ref=own, dst_ref=buf.at[rep], send_sem=send.at[j - 1], recv_sem=recv.at[j - 1],
                device_id=((rep + j) % reps, me), device_id_type=MESH,
            )
            for j in range(1, reps)
        ]

    def each(self, sent, act):
        for j, copy in enumerate(self.copies, 1):
            if self.neighbours or j not in (1, self.reps - 1):
                act(copy)
            else:
                end = self.reps - 1 if (j == 1) == sent else 0

                @pl.when(self.rep == end)
                def _(copy=copy):
                    act(copy)

    def start(self):
        self.each(True, lambda copy: copy.start())

    def finish(self):
        self.each(True, lambda copy: copy.wait_send())
        self.each(False, lambda copy: copy.wait_recv())


def on_ends(low, high):
    pl.when(lax.axis_index("rep") == 0)(low)
    pl.when(lax.axis_index("rep") == lax.axis_size("rep") - 1)(high)


class Spread:
    def __init__(self, oth, col, own, send, recv, psend, precv, asend, arecv, lsem):
        self.oth, self.col, self.own, self.send, self.recv = oth, col, own, send, recv
        self.psend, self.precv, self.asend, self.arecv, self.lsem = psend, precv, asend, arecv, lsem
        self.rep, self.me, self.reps = lax.axis_index("rep"), lax.axis_index("shard"), lax.axis_size("rep")
        self.core = self.me % 2
        self.blocks = range(lax.axis_size("shard") // 2)

    @staticmethod
    def semaphores(shards, reps):
        n = PlaneGather.copies(shards)
        dma = lambda *k: pltpu.SemaphoreType.DMA(k)
        return [dma(reps - 1, n), dma(reps - 1, n), *[dma(2, shards // 2)] * 4, dma(reps - 1)]

    def gather(self, j):
        return PlaneGather(self.oth.at[j - 1], self.col.at[(self.rep + j) % self.reps], self.send.at[j - 1], self.recv.at[j - 1])

    def own_copy(self, j):
        return pltpu.make_async_copy(self.col.at[(self.rep + j) % self.reps], self.oth.at[j - 1, self.me], self.lsem.at[j - 1])

    def begin(self, j):
        self.gather(j).start()
        self.own_copy(j).start()

    def forward(self, j):
        self.gather(j).forward(0)

    def end(self, j):
        gather = self.gather(j)
        for step in range(1, gather.steps):
            gather.forward(step)
        gather.finish()
        self.own_copy(j).wait()

    def straight(self, up, b):
        at, way = 2 * b + self.core, self.reps - 2 if up else 0
        return pltpu.make_async_remote_copy(
            src_ref=self.own.at[at], dst_ref=self.oth.at[way, at], send_sem=self.psend.at[up, b], recv_sem=self.precv.at[up, b],
            device_id=((self.rep + (1 if up else self.reps - 1)) % self.reps, self.me), device_id_type=MESH,
        )

    def across(self, up, b):
        at, way = 2 * b + self.core, self.reps - 2 if up else 0
        return pltpu.make_async_remote_copy(
            src_ref=self.oth.at[way, at], dst_ref=self.oth.at[way, at], send_sem=self.asend.at[up, b], recv_sem=self.arecv.at[up, b],
            device_id=(self.rep, flip(self.me, 1)), device_id_type=MESH,
        )

    def sends(self, up):
        return self.rep < self.reps - 1 if up else self.rep > 0

    def gets(self, up):
        return self.rep > 0 if up else self.rep < self.reps - 1

    def start_straight(self):
        for up in (0, 1):
            @pl.when(self.sends(up))
            def _(up=up):
                for b in self.blocks:
                    self.straight(up, b).start()

    def sent_straight(self):
        for up in (0, 1):
            @pl.when(self.sends(up))
            def _(up=up):
                for b in self.blocks:
                    self.straight(up, b).wait_send()

    def got_straight(self, up):
        @pl.when(self.gets(up))
        def _():
            for b in self.blocks:
                self.straight(up, b).wait_recv()

    def start_across(self, up):
        @pl.when(self.gets(up))
        def _():
            for b in self.blocks:
                self.across(up, b).start()

    def end_across(self, up):
        @pl.when(self.gets(up))
        def _():
            for b in self.blocks:
                self.across(up, b).wait()


def rotate(v, cosine, sine, sign):
    lane = lax.broadcasted_iota(jnp.int32, v.shape, 1) % HEAD_SIZE
    half = HEAD_SIZE // 2
    low = lane < half
    other = jnp.where(low, -pltpu.roll(v, LANES - half, 1), pltpu.roll(v, half, 1))
    return v * cosine + sign * other * sine

def two_heads(v):
    low = lax.broadcasted_iota(jnp.int32, v.shape, 1) < HEAD_SIZE
    zero = jnp.zeros_like(v)
    return jnp.concatenate([jnp.where(low, v, zero), jnp.where(low, zero, v)], axis=0)

def one_head_twice(pair, odd):
    high = lax.broadcasted_iota(jnp.int32, pair.shape, 1) // HEAD_SIZE
    wide = pair.astype(f32)
    return jnp.where(high == odd, wide, pltpu.roll(wide, HEAD_SIZE, 1)).astype(pair.dtype)

def probabilities(query2, keys, prefix_len):
    rows = query2.shape[0] // 2
    raw = dot(query2, keys, ((1,), (1,)))
    row = lax.broadcasted_iota(jnp.int32, raw.shape, 0) % rows
    col = lax.broadcasted_iota(jnp.int32, raw.shape, 1)
    scores = jnp.where((col <= row) | (col < prefix_len), raw * score_scale, masked_value)
    weights = jnp.exp(scores - jnp.max(scores, axis=-1, keepdims=True))
    return weights / jnp.sum(weights, axis=-1, keepdims=True)

def lanes(j, count=1):
    return pl.ds(pl.multiple_of(j * LANES * count, LANES), LANES * count)

def front_kernel(spread, prefix_ref, tok_ref, routes_ref, cos_ref, sin_ref, wq_hbm, wk_hbm, wv_hbm, wo_hbm, ws_hbm, cot_ref,
                 wall_out, cown_out, ccol_out, q_out, k_out, v_out, att_out, hid_out, x_out, gates_out, n1_out,
                 wbuf, qkv_ref, send, recv, csend, crecv, zsend, zrecv, lsem, osem):
    count, width = tok_ref.shape
    kv_width = k_out.shape[1]
    experts = gates_out.shape[0]
    shards, depth, total = wbuf.shape
    me = lax.axis_index("shard")
    own, at = [], 0
    for i, part in enumerate((wq_hbm, wk_hbm, wv_hbm, wo_hbm, ws_hbm)):
        own.append(pltpu.make_async_copy(part, wbuf.at[me, :, at:at + part.shape[1]], osem.at[i]))
        own[-1].start()
        at += part.shape[1]
    greet(spread)
    gather = PlaneGather(wbuf, wbuf.at[me], send, recv)
    for copy in own:
        copy.wait()
    gather.start()
    far = RepSends(ccol_out, cot_ref, zsend, zrecv, False)
    if spread:
        far.start()
    near = PlaneGather(cown_out, cot_ref, csend, crecv)
    own_cot = pltpu.make_async_copy(cot_ref, cown_out.at[me], lsem.at[2])
    own_cot.start()
    inputs = tok_ref[...].astype(f32)
    scaled = inputs * norm_scale(inputs)
    for step in range(gather.steps):
        gather.forward(step)
    gather.finish()
    near.start()
    keep = pltpu.make_async_copy(wbuf, wall_out, lsem.at[1])
    keep.start()
    cut = [0, width, width + kv_width, width + 2 * kv_width, 2 * width + 2 * kv_width]
    small = wbuf[:, :, cut[4]:].reshape(shards * depth, total - cut[4])
    wide = small.astype(f32).T
    gain_one, gain_two = wide[experts:experts + 1], wide[experts + 1:experts + 2]
    n1_out[...] = (scaled * gain_one).astype(bf16)

    def project(j, carry):
        w = wbuf[:, :, lanes(j, 2)].reshape(shards * depth, 2 * LANES)
        qkv_ref[:, lanes(j, 2)] = dot(n1_out[...], w)
        return carry
    lax.fori_loop(0, cut[3] // (2 * LANES), project, 0)
    cosine, sine = cos_ref[...], sin_ref[...]
    for j in range(width // LANES):
        q_out[:, j * LANES:(j + 1) * LANES] = rotate(qkv_ref[:, j * LANES:(j + 1) * LANES], cosine, sine, 1.0).astype(bf16)
    for j in range(kv_width // LANES):
        at = slice(cut[1] + j * LANES, cut[1] + (j + 1) * LANES)
        k_out[:, j * LANES:(j + 1) * LANES] = rotate(qkv_ref[:, at], cosine, sine, 1.0).astype(bf16)
    v_out[...] = qkv_ref[:, cut[2]:cut[3]].astype(bf16)
    prefix_len = prefix_ref[0]

    near.forward(0)

    def head(j, carry):
        keys = one_head_twice(k_out[:, lanes(j // 2)], j % 2)
        values = one_head_twice(v_out[:, lanes(j // 2)], j % 2)
        prob = probabilities(two_heads(q_out[:, lanes(j)]), keys, prefix_len)
        both = dot(prob.astype(bf16), values)
        low = lax.broadcasted_iota(jnp.int32, (count, LANES), 1) < HEAD_SIZE
        att_out[:, lanes(j)] = jnp.where(low, both[:count], both[count:]).astype(bf16)
        return carry
    lax.fori_loop(0, KEY_VALUE_HEADS, head, 0)
    for step in range(1, near.steps):
        near.forward(step)

    def project_out(j, carry):
        w = wbuf[:, :, pl.ds(pl.multiple_of(cut[3] + j * 2 * LANES, LANES), 2 * LANES)].reshape(shards * depth, 2 * LANES)
        qkv_ref[:, lanes(j, 2)] = dot(att_out[...], w)
        return carry
    lax.fori_loop(0, width // (2 * LANES), project_out, 0)
    hidden = inputs + branch_scale * qkv_ref[:, :width]
    hid_out[...] = hidden
    x = (hidden * norm_scale(hidden) * gain_two).astype(bf16)
    x_out[...] = x
    logits = dot(x, small).T[:experts]
    expert = lax.broadcasted_iota(jnp.int32, (experts, count), 0)
    named = expert < 0
    for k in range(routes_ref.shape[0]):
        named = named | (routes_ref[k:k + 1, :] == expert)
    top = jnp.max(jnp.where(named, logits, masked_value), axis=0, keepdims=True)
    weights = jnp.where(named, jnp.exp(jnp.where(named, logits - top, 0.0)), 0.0)
    gates_out[...] = weights / jnp.sum(weights, axis=0, keepdims=True)
    keep.wait()
    near.finish()
    own_cot.wait()
    if spread:
        far.finish()

def front(tokens, prefix, routes, mine, cot, cosine, sine, experts, kv_width, spread):
    count, width = tokens.shape
    shards, reps = lax.axis_size("shard"), lax.axis_size("rep")
    depth, total = tokens.shape[1] // shards, sum(part.shape[1] for part in mine)
    v = pl.BlockSpec(memory_space=pltpu.VMEM)
    any_ = pl.BlockSpec(memory_space=pl.ANY)
    sds = jax.ShapeDtypeStruct
    n = PlaneGather.copies(shards)
    return pl.pallas_call(
        functools.partial(front_kernel, spread),
        out_shape=[
            sds((shards, depth, total), bf16), sds((shards, count, width), bf16), sds((reps, count, width), bf16), sds((count, width), bf16), sds((count, kv_width), bf16), sds((count, kv_width), bf16),
            sds((count, width), bf16), sds((count, width), f32), sds((count, width), bf16), sds((experts, count), f32), sds((count, width), bf16),
        ],
        in_specs=[pl.BlockSpec(memory_space=pltpu.SMEM), v, v, v, v] + [any_] * 6,
        out_specs=[any_] * 3 + [v] * 8,
        scratch_shapes=[
            pltpu.VMEM((shards, depth, total), bf16), pltpu.VMEM((count, width + 2 * kv_width), f32),
            *[pltpu.SemaphoreType.DMA((k,)) for k in (n, n, n, n, reps, reps, 3, 5)],
        ],
        compiler_params=pltpu.CompilerParams(vmem_limit_bytes=60 << 20, has_side_effects=True, collective_id=1),
        name="front",
    )(prefix, tokens, routes, cosine, sine, *mine, cot)

class PlaneReduce:
    def __init__(self, mine, theirs, from_core, from_chip, csend, crecv, send, recv):
        self.mine, self.theirs, self.from_core, self.from_chip = mine, theirs, from_core, from_chip
        self.csend, self.crecv, self.send, self.recv = csend, crecv, send, recv
        self.rep, self.me = lax.axis_index("rep"), lax.axis_index("shard")
        self.core = self.me % 2
        self.bits = [1 << i for i in range(1, lax.axis_size("shard").bit_length() - 1)]
        self.steps = len(self.bits)

    def owner(self, core, u):
        at = flip(self.me, 1) if core else self.me
        of = (1 - self.core) if core else self.core
        for step in range(self.steps):
            if u >> step & 1:
                at = turned(at, of, step, self.bits)
        return at

    def core_copy(self, u):
        return pltpu.make_async_remote_copy(
            src_ref=self.theirs.at[u], dst_ref=self.from_core.at[u], send_sem=self.csend.at[u], recv_sem=self.crecv.at[u],
            device_id=(self.rep, flip(self.me, 1)), device_id_type=MESH,
        )

    def slot(self, step, u):
        return (1 << self.steps) - (1 << (self.steps - step)) + (u >> (step + 1))

    def chip_copy(self, step, u):
        slot = self.slot(step, u)
        return pltpu.make_async_remote_copy(
            src_ref=self.mine.at[u], dst_ref=self.from_chip.at[slot], send_sem=self.send.at[slot], recv_sem=self.recv.at[slot],
            device_id=(self.rep, turned(self.me, self.core, step, self.bits)), device_id_type=MESH,
        )

    def total(self, u, before, rows):
        whole = self.mine[u, rows].astype(f32) + self.from_core[u, rows].astype(f32)
        for step in range(before):
            whole = whole + self.from_chip[self.slot(step, u), rows].astype(f32)
        return whole

    def send_on(self, step, u):
        self.core_copy(u).wait_recv()
        count = self.mine.shape[1]
        piece = 32

        def add(i, carry):
            rows = pl.ds(pl.multiple_of(i * piece, piece), piece)
            self.mine[u, rows] = self.total(u, step, rows).astype(bf16)
            return carry
        lax.fori_loop(0, count // piece, add, 0)
        self.chip_copy(step, u).start()

    def group(self, step):
        return [u for u in range(1 << self.steps) if u % (2 << step) == 1 << step]

    def arrive(self, step):
        for u in self.group(step):
            self.chip_copy(step, u).wait_recv()

    def advance(self, step):
        if step < self.steps:
            if step:
                self.arrive(step - 1)
            for u in self.group(step):
                self.send_on(step, u)

    def last(self, out, plus=None):
        self.arrive(self.steps - 1)
        self.core_copy(0).wait_recv()
        count = self.mine.shape[1]
        piece = 32

        def add(i, carry):
            rows = pl.ds(pl.multiple_of(i * piece, piece), piece)
            whole = self.total(0, self.steps, rows)
            out[rows] = (whole if plus is None else whole + plus[rows]).astype(out.dtype)
            return carry
        lax.fori_loop(0, count // piece, add, 0)

    def finish(self):
        for u in range(1 << self.steps):
            self.core_copy(u).wait_send()
        for step in range(self.steps):
            for u in self.group(step):
                self.chip_copy(step, u).wait_send()


def own_kernel(spread, nb, x_ref, gates_ref, c_hbm, ccol_hbm, wg_hbm, wu_hbm, wd_hbm,
               xown_out, xcol_out, gown_out, gcol_out, back_out, dg_out, mix_out, coth_out,
               wg, wu, wd, xb, cb, xg_ref, cg_ref, sg_ref, y_ref, ds_ref, mine, theirs, mix, from_core, from_chip,
               gown, gcol, dgs, dgr,
               xs, xr, zxs, zxr, zgs, zgr, gs, gr, dss, dsr, css, csr, hs, hr, wsem, bsem, lsem, msem, *csems):
    count, width = x_ref.shape
    local, _, hidden = wg.shape
    rep, me = lax.axis_index("rep"), lax.axis_index("shard")
    shards = lax.axis_size("shard")
    first = me * local
    greet(spread)
    near = PlaneGather(xown_out, x_ref, xs, xr)
    near.start()
    gown[me] = gates_ref[...]

    def peer(j):
        return (rep, (me + j) % shards)

    gate_sends = [
        pltpu.make_async_remote_copy(
            src_ref=gates_ref, dst_ref=gown.at[me], send_sem=gs.at[j - 1], recv_sem=gr.at[j - 1],
            device_id=peer(j), device_id_type=MESH,
        )
        for j in range(1, shards)
    ]
    for copy in gate_sends:
        copy.start()
    far = [RepSends(xcol_out, x_ref, zxs, zxr, False), RepSends(gcol, gates_ref, zgs, zgr, True)] if spread else []
    for sends in far:
        sends.start()
    cots = Spread(coth_out, ccol_hbm, c_hbm, *csems)
    reps = lax.axis_size("rep")
    if spread:
        cots.start_straight()
    own_x = pltpu.make_async_copy(x_ref, xown_out.at[me], lsem)
    own_x.start()
    weights = [pltpu.make_async_copy(a, b, wsem.at[i]) for i, (a, b) in enumerate(((wg_hbm, wg), (wu_hbm, wu), (wd_hbm, wd)))]
    for copy in weights:
        copy.start()
    reduce = PlaneReduce(mine, theirs, from_core, from_chip, css, csr, hs, hr)
    for copy in gate_sends:
        copy.wait_recv()
    order = list(range(1 << reduce.steps))
    half = nb // 2
    dg_sends, mixes = [], []

    def fetch(at, slot):
        return (pltpu.make_async_copy(xown_out.at[at], xb.at[slot], bsem.at[0, slot]),
                pltpu.make_async_copy(c_hbm.at[at], cb.at[slot], bsem.at[1, slot]))

    chunks = [order[q:q + half] for q in range(0, len(order), half)]
    forwarded = 0
    for q, chunk in enumerate(chunks):
        plan = [(core, u) for u in chunk for core in (0, 1)]
        owners = [reduce.owner(core, u) for core, u in plan]
        while forwarded < chunk[-1].bit_length():
            near.forward(forwarded)
            forwarded += 1
        if not q:
            own_x.wait()
        for u in chunk:
            near.core_copy(u).wait_recv()
        for copy in fetch(owners[0], 0):
            copy.start()
        for b in range(nb):
            if b + 1 < nb:
                for copy in fetch(owners[b + 1], (b + 1) % 2):
                    copy.start()
            for copy in fetch(owners[b], b % 2):
                copy.wait()
            gather_block(xb[b % 2], cb[b % 2], gown[owners[b]], first, local, xg_ref, cg_ref, sg_ref, b * CAP)
        if not q:
            for copy in weights:
                copy.wait()

        def expert(l, carry):
            inner, raw, d_gate, d_up, scaled = expert_parts(xg_ref[l], cg_ref[l], sg_ref[l], wg[l], wu[l], wd[l])
            ds_ref[l] = branch_scale * jnp.sum(inner * raw, axis=1, keepdims=True)
            rows = pl.ds(pl.multiple_of(l * CAP, CAP), CAP)
            out = dot(scaled, wd[l]).astype(bf16)
            d_in = (dot(d_gate, wg[l], ((1,), (1,))) + dot(d_up, wu[l], ((1,), (1,)))).astype(bf16)
            for b in range(nb):
                y_ref[b, rows, :width] = out[b * CAP:(b + 1) * CAP]
                y_ref[b, rows, width:] = d_in[b * CAP:(b + 1) * CAP]
            return carry
        lax.fori_loop(0, local, expert, 0)
        if q + 1 < len(chunks):
            while forwarded < chunks[q + 1][-1].bit_length():
                near.forward(forwarded)
                forwarded += 1
        if spread:
            if not q:
                cots.begin(2)
            else:
                cots.forward(2)
        for b in range(nb):
            core, u = plan[b]
            parts = slot_one_hot(slot_ranks(gown[owners[b]]), first, local)
            table = jnp.concatenate(parts, axis=0).astype(bf16)
            both = dot(table, y_ref[b], ((0,), (0,))).astype(bf16)
            mix[core, u] = both[:, :width]
            mixes.append(pltpu.make_async_copy(mix.at[core, u], mix_out.at[owners[b]], msem.at[core, u]))
            mixes[-1].start()
            (theirs if core else mine)[u] = both[:, width:]
            if core:
                reduce.core_copy(u).start()
            dgs[owners[b]] = jnp.concatenate(
                [jnp.sum(parts[l] * ds_ref[l, b * CAP:(b + 1) * CAP], axis=0, keepdims=True) for l in range(local)], axis=0
            )
        for u in chunk:
            if u % 2:
                reduce.send_on(0, u)
    for j in range(1, shards):
        copy = pltpu.make_async_remote_copy(
            src_ref=dgs.at[(me + j) % shards], dst_ref=dgr.at[me], send_sem=dss.at[j - 1], recv_sem=dsr.at[j - 1],
            device_id=peer(j), device_id_type=MESH,
        )
        copy.start()
        dg_sends.append(copy)
    dgr[me] = dgs[me]
    gown_out[...] = gown[...]
    for step in range(1, reduce.steps):
        reduce.advance(step)
    reduce.last(back_out)
    for copy in dg_sends:
        copy.wait()
    dg_out[...] = dgr[...]
    if spread:
        cots.end(2)
        cots.got_straight(0)
        cots.got_straight(1)
        cots.sent_straight()
    reduce.finish()
    for copy in mixes:
        copy.wait()
    near.sent()
    for copy in gate_sends:
        copy.wait_send()
    for sends in far:
        sends.finish()
    if spread:
        gcol_out[...] = gcol[...]


def moe_own(x, gates, c, ccol, wg, wu, wd, spread, nb=4):
    count, width = x.shape
    local, _, hidden = wg.shape
    shards, reps = lax.axis_size("shard"), lax.axis_size("rep")
    experts = local * shards
    v = pl.BlockSpec(memory_space=pltpu.VMEM)
    any_ = pl.BlockSpec(memory_space=pl.ANY)
    sds = jax.ShapeDtypeStruct
    n = PlaneGather.copies(shards)
    rows = nb * CAP
    half = shards // 2
    dma = lambda *k: pltpu.SemaphoreType.DMA(k)
    return pl.pallas_call(
        functools.partial(own_kernel, spread, nb),
        out_shape=[
            sds((shards, count, width), bf16), sds((reps, count, width), bf16), sds((shards, experts, count), f32),
            sds((reps, experts, count), f32), sds((count, width), f32), sds((shards, local, count), f32),
            sds((shards, count, width), bf16), sds((max(reps - 1, 1), shards, count, width) if spread else (1, 1, 16, LANES), bf16),
        ],
        in_specs=[v, v, any_, any_, any_, any_, any_],
        out_specs=[any_, any_, v, v, v, v, any_, any_],
        scratch_shapes=[
            pltpu.VMEM(wg.shape, bf16), pltpu.VMEM(wu.shape, bf16), pltpu.VMEM(wd.shape, bf16),
            pltpu.VMEM((2, count, width), bf16), pltpu.VMEM((2, count, width), bf16),
            pltpu.VMEM((local, rows, width), bf16), pltpu.VMEM((local, rows, width), bf16), pltpu.VMEM((local, rows, 1), f32),
            pltpu.VMEM((nb, local * CAP, 2 * width), bf16), pltpu.VMEM((local, rows, 1), f32),
            *[pltpu.VMEM((k, count, width), bf16) for k in (half, half)], pltpu.VMEM((2, half, count, width), bf16),
            *[pltpu.VMEM((k, count, width), bf16) for k in (half, half - 1)],
            pltpu.VMEM((shards, experts, count), f32), pltpu.VMEM((reps, experts, count), f32),
            pltpu.VMEM((shards, local, count), f32), pltpu.VMEM((shards, local, count), f32),
            dma(n), dma(n), dma(reps), dma(reps), dma(reps), dma(reps), dma(shards), dma(shards), dma(shards), dma(shards),
            dma(half), dma(half), dma(half), dma(half), dma(3), dma(2, 2), pltpu.SemaphoreType.DMA, dma(2, half),
            *Spread.semaphores(shards, reps),
        ],
        compiler_params=pltpu.CompilerParams(vmem_limit_bytes=60 << 20, has_side_effects=True, collective_id=2),
        name="own_experts",
    )(x, gates, c, ccol, wg, wu, wd)

def norm_backward(rows, scaling, gain, upstream):
    weighted = upstream * gain
    inner_mean = jnp.mean(weighted * rows, axis=-1, keepdims=True)
    gradient = scaling * weighted - rows * (scaling * scaling * scaling) * inner_mean
    return gradient, jnp.sum(upstream * rows * scaling, axis=0, keepdims=True)


def back_kernel(prefix_ref, tok_ref, cot_ref, cos_ref, sin_ref, w_ref, q_ref, k_ref, v_ref, att_ref, n1_ref, x_ref,
                hid_ref, gates_ref, dg_ref, back_ref, dtok_out, shares_out, dqkv_ref, datt_ref, dproj_ref):
    count, width = tok_ref.shape
    kv_width = k_ref.shape[1]
    experts = gates_ref.shape[0]
    shards, depth, total = w_ref.shape
    rows = shards * depth
    cut = [0, width, width + kv_width, width + 2 * kv_width, 2 * width + 2 * kv_width]
    small = w_ref[:, :, cut[4]:].reshape(rows, total - cut[4])
    wide = small.astype(f32).T
    gain_one, gain_two = wide[experts:experts + 1], wide[experts + 1:experts + 2]
    hidden = hid_ref[...]
    gates, d_gates = gates_ref[...], dg_ref[...]
    d_logits = gates * (d_gates - jnp.sum(gates * d_gates, axis=0, keepdims=True))
    none = jnp.zeros((LANES - experts, count), f32)
    d_logits = jnp.concatenate([d_logits, none], axis=0).T.astype(bf16)
    d_normed_two = back_ref[...] + dot(d_logits, small, ((1,), (1,)))
    d_hidden, d_gain_two = norm_backward(hidden, norm_scale(hidden), gain_two, d_normed_two)
    d_hidden = d_hidden + cot_ref[...].astype(f32)
    dtok_out[...] = d_hidden
    dproj_ref[...] = (branch_scale * d_hidden).astype(bf16)
    tile = 2 * LANES

    def out_tile(j, carry):
        grad = dot(att_ref[...], dproj_ref[:, lanes(j, 2)], ((0,), (0,))).astype(bf16)
        at = pl.ds(pl.multiple_of(cut[3] + j * tile, LANES), tile)
        shares_out[:, :, at] = grad.reshape(shards, depth, tile)
        return carry
    lax.fori_loop(0, width // tile, out_tile, 0)
    datt_ref[...] = dot(dproj_ref[...], w_ref[:, :, cut[3]:cut[4]].reshape(rows, width), ((1,), (1,))).astype(bf16)
    cosine, sine = cos_ref[...], sin_ref[...]
    prefix_len = prefix_ref[0]
    low = lax.broadcasted_iota(jnp.int32, (count, LANES), 1) < HEAD_SIZE

    def pair(p, carry):
        at_k = pl.ds(pl.multiple_of(cut[1] + p * LANES, LANES), LANES)
        at_v = pl.ds(pl.multiple_of(cut[2] + p * LANES, LANES), LANES)
        d_keys, d_values = [], []
        for odd in range(2):
            j = 2 * p + odd
            keys = one_head_twice(k_ref[:, lanes(p)], odd)
            values = one_head_twice(v_ref[:, lanes(p)], odd)
            query2, d_att2 = two_heads(q_ref[:, lanes(j)]), two_heads(datt_ref[:, lanes(j)])
            prob = probabilities(query2, keys, prefix_len)
            d_value = dot(prob.astype(bf16), d_att2, ((0,), (0,)))
            d_prob = dot(d_att2, values, ((1,), (1,)))
            weighted = jnp.sum(prob * d_prob, axis=-1, keepdims=True)
            d_score = (prob * (d_prob - weighted) * score_scale).astype(bf16)
            d_query = dot(d_score, keys)
            d_query = jnp.where(low, d_query[:count], d_query[count:])
            dqkv_ref[:, lanes(j)] = rotate(d_query, cosine, sine, -1.0).astype(bf16)
            d_key = dot(d_score, query2, ((0,), (0,)))
            d_keys.append(d_key + pltpu.roll(d_key, HEAD_SIZE, 1))
            d_values.append(d_value + pltpu.roll(d_value, HEAD_SIZE, 1))
        dqkv_ref[:, at_k] = rotate(jnp.where(low, *d_keys), cosine, sine, -1.0).astype(bf16)
        dqkv_ref[:, at_v] = jnp.where(low, *d_values).astype(bf16)
        return carry
    lax.fori_loop(0, KEY_VALUE_HEADS // 2, pair, 0)

    def in_tile(j, carry):
        grad = dot(n1_ref[...], dqkv_ref[:, lanes(j, 2)], ((0,), (0,))).astype(bf16)
        shares_out[:, :, lanes(j, 2)] = grad.reshape(shards, depth, tile)
        return carry
    lax.fori_loop(0, cut[3] // tile, in_tile, 0)
    d_normed_one = dot(dqkv_ref[...], w_ref[:, :, :cut[3]].reshape(rows, cut[3]), ((1,), (1,)))
    inputs = tok_ref[...].astype(f32)
    d_inputs, d_gain_one = norm_backward(inputs, norm_scale(inputs), gain_one, d_normed_one)
    dtok_out[...] += d_inputs
    row = lax.broadcasted_iota(jnp.int32, (LANES, rows), 0)
    gains = jnp.where(row == experts, d_gain_one, jnp.where(row == experts + 1, d_gain_two, 0.0)).T
    d_small = (dot(x_ref[...], d_logits, ((0,), (0,))) + gains).astype(bf16)
    shares_out[:, :, cut[4]:] = d_small.reshape(shards, depth, total - cut[4])


def attention_back(prefix, tokens, cot, cosine, sine, packed, query, keys, values, attended, n1, x, hidden, gates, d_gates, back):
    count, width = tokens.shape
    v = pl.BlockSpec(memory_space=pltpu.VMEM)
    sds = jax.ShapeDtypeStruct
    return pl.pallas_call(
        back_kernel,
        out_shape=[sds((count, width), f32), sds(packed.shape, bf16)],
        in_specs=[pl.BlockSpec(memory_space=pltpu.SMEM)] + [v] * 15,
        out_specs=[v] * 2,
        scratch_shapes=[
            pltpu.VMEM((count, width + 2 * keys.shape[1]), bf16), pltpu.VMEM((count, width), bf16), pltpu.VMEM((count, width), bf16),
        ],
        compiler_params=pltpu.CompilerParams(vmem_limit_bytes=60 << 20),
        name="attention_back",
    )(prefix, tokens, cot, cosine, sine, packed, query, keys, values, attended, n1, x, hidden, gates, d_gates, back)

def spread_kernel(nb, xown_hbm, cown_hbm, xcol_hbm, ccol_hbm, gown_ref, gcol_ref, wg_hbm, wu_hbm, wd_hbm, coth_in,
                  xoth_hbm, coth_hbm, og_hbm, ou_hbm, od_hbm, glast_ref,
                  xbuf, cbuf, wg, wu, wd, ag, au, ad, xg_ref, cg_ref, sg_ref, goth, send, recv, bsem, wsem, *sems):
    xsems, csems = sems[:7], sems[7:]
    local = wg.shape[0]
    shards = gown_ref.shape[0]
    rep, me = lax.axis_index("rep"), lax.axis_index("shard")
    reps = lax.axis_size("rep")
    first = me * local
    chunks = shards // nb

    xs = Spread(xoth_hbm, xcol_hbm, xown_hbm, *xsems)
    cs = Spread(coth_hbm, ccol_hbm, cown_hbm, *csems)
    both = (xs, cs)

    def each(act, j):
        for one in both:
            act(one, j)

    def gate_gathers():
        return [PlaneGather(goth.at[j - 1], gcol_ref.at[(rep + j) % reps], send.at[j - 1], recv.at[j - 1]) for j in range(1, reps)]

    def fetch(x, c, q, slot):
        return (pltpu.make_async_copy(x.at[pl.ds(q * nb, nb)], xbuf.at[slot], bsem.at[0, slot]),
                pltpu.make_async_copy(c.at[pl.ds(q * nb, nb)], cbuf.at[slot], bsem.at[1, slot]))

    def replica(x, c, g, midway, last):
        for copy in fetch(x, c, 0, 0):
            copy.start()

        def chunk(q, carry):
            slot = lax.rem(q, 2)

            @pl.when(q + 1 < chunks)
            def _():
                for copy in fetch(x, c, q + 1, 1 - slot):
                    copy.start()
            for copy in fetch(x, c, q, slot):
                copy.wait()

            def block(b, carry):
                gather_block(xbuf[slot, b], cbuf[slot, b], g[q * nb + b], first, local, xg_ref, cg_ref, sg_ref,
                             pl.multiple_of(b * CAP, CAP))
                return carry
            lax.fori_loop(0, nb, block, 0)

            def expert(l, carry):
                add_expert(l, xg_ref, cg_ref, sg_ref, wg, wu, wd, ag, au, ad)

                @pl.when((q == chunks // 2) & (l == 0))
                def _():
                    midway()
                return carry
            lax.fori_loop(0, local, expert, 0)
            return carry
        lax.fori_loop(0, chunks, chunk, 0)
        last()

    greet(True)
    xs.begin(2)
    for j in range(1, reps):
        goth[j - 1, me] = gcol_ref[(rep + j) % reps]
    for gather in gate_gathers():
        gather.start()
    xs.start_straight()
    for up in (0, 1):
        cs.start_across(up)
    weights = [pltpu.make_async_copy(a, b, wsem.at[i]) for i, (a, b) in enumerate(((wg_hbm, wg), (wu_hbm, wu), (wd_hbm, wd)))]
    for copy in weights:
        copy.start()
    ag[...] = jnp.zeros_like(ag)
    au[...] = jnp.zeros_like(au)
    ad[...] = jnp.zeros_like(ad)
    for copy in weights:
        copy.wait()

    def midway_own():
        xs.forward(2)
        for gather in gate_gathers():
            gather.forward(0)
        on_ends(lambda: each(Spread.begin, reps - 1), lambda: each(Spread.begin, 1))

    def last_own():
        xs.end(2)
        for gather in gate_gathers():
            for step in range(1, gather.steps):
                gather.forward(step)
        for gather in gate_gathers():
            gather.finish()
        for up in (0, 1):
            cs.end_across(up)

    def midway_two():
        on_ends(lambda: each(Spread.forward, reps - 1), lambda: each(Spread.forward, 1))
        xs.got_straight(1)
        xs.start_across(1)

        @pl.when(rep == 0)
        def _():
            xs.got_straight(0)
            xs.start_across(0)

    def last_two():
        xs.end_across(1)
        pl.when(rep == 0)(lambda: xs.end_across(0))

    def midway_three():
        @pl.when(rep > 0)
        def _():
            xs.got_straight(0)
            xs.start_across(0)

    def last_three():
        on_ends(lambda: each(Spread.end, reps - 1), lambda: each(Spread.end, 1))
        pl.when(rep > 0)(lambda: xs.end_across(0))

    replica(xown_hbm, cown_hbm, gown_ref, midway_own, last_own)
    replica(xoth_hbm.at[1], coth_hbm.at[1], goth.at[1], midway_two, last_two)
    third, left = late_places(rep, reps)
    replica(xoth_hbm.at[third], coth_hbm.at[third], goth.at[third], midway_three, last_three)
    xs.sent_straight()
    glast_ref[...] = goth[left]
    outs = [pltpu.make_async_copy(a, b, wsem.at[i]) for i, (a, b) in enumerate(((ag, og_hbm), (au, ou_hbm), (ad, od_hbm)))]
    for copy in outs:
        copy.start()
    for copy in outs:
        copy.wait()


def moe_spread_sums(xown, cown, xcol, ccol, coth, gown, gcol, wg, wu, wd, nb=4):
    shards, count, width = xown.shape
    reps = xcol.shape[0]
    local, _, hidden = wg.shape
    any_ = pl.BlockSpec(memory_space=pl.ANY)
    v = pl.BlockSpec(memory_space=pltpu.VMEM)
    rows = nb * CAP
    n = PlaneGather.copies(shards)
    slots = reps * shards * local * CAP
    outs = pl.pallas_call(
        functools.partial(spread_kernel, nb),
        out_shape=[jax.ShapeDtypeStruct((reps - 1, shards, count, width), bf16)] * 2
        + [jax.ShapeDtypeStruct(w.shape, f32) for w in (wg, wu, wd)] + [jax.ShapeDtypeStruct(gown.shape, f32)],
        in_specs=[any_, any_, any_, any_, v, v, any_, any_, any_, any_],
        input_output_aliases={9: 1},
        out_specs=[any_] * 5 + [v],
        scratch_shapes=[
            pltpu.VMEM((2, nb, count, width), bf16), pltpu.VMEM((2, nb, count, width), bf16),
            pltpu.VMEM(wg.shape, bf16), pltpu.VMEM(wu.shape, bf16), pltpu.VMEM(wd.shape, bf16),
            pltpu.VMEM(wg.shape, f32), pltpu.VMEM(wu.shape, f32), pltpu.VMEM(wd.shape, f32),
            pltpu.VMEM((local, rows, width), bf16), pltpu.VMEM((local, rows, width), bf16), pltpu.VMEM((local, rows, 1), f32),
            pltpu.VMEM((reps - 1, shards, *gown.shape[1:]), f32),
            pltpu.SemaphoreType.DMA((reps - 1, n)), pltpu.SemaphoreType.DMA((reps - 1, n)),
            pltpu.SemaphoreType.DMA((2, 2)), pltpu.SemaphoreType.DMA((3,)),
            *Spread.semaphores(shards, reps), *Spread.semaphores(shards, reps),
        ],
        compiler_params=pltpu.CompilerParams(vmem_limit_bytes=60 << 20, has_side_effects=True, collective_id=3),
        cost_estimate=pl.CostEstimate(
            flops=12 * slots * width * hidden, transcendentals=slots * hidden, bytes_accessed=4 * reps * shards * count * width
        ),
        name="spread_expert_sums",
    )(xown, cown, xcol, ccol, gown, gcol, wg, wu, wd, coth)
    return outs[0], outs[1], outs[5], outs[2:5]

def rotary_tables(count):
    half = HEAD_SIZE // 2
    inverse = np.exp(np.arange(half) * (-2.0 * math.log(10000.0) / HEAD_SIZE))
    angles = np.tile(np.arange(count)[:, None] * inverse[None, :], (1, LANES // half))
    return np.cos(angles).astype(np.float32), np.sin(angles).astype(np.float32)


def pack_small(w_router, norm_attn, norm_moe):
    small = jnp.concatenate([w_router, norm_attn[:, None], norm_moe[:, None]], axis=1)
    return jnp.pad(small, ((0, 0), (0, LANES - small.shape[1])))


def body(
    tokens, prefix, routes, cotangent, w_query, key_weight, value_weight, w_out,
    norm_attn, norm_moe, w_router, w_gate, w_up, w_down,
):
    count, width = tokens.shape
    local = w_gate.shape[0]
    shards, reps = lax.axis_size("shard"), lax.axis_size("rep")
    experts = local * shards
    kv_width = key_weight.shape[1]
    spread = reps == GATHERED_REPLICAS
    cosine, sine = rotary_tables(count)
    packed_own = (w_query, key_weight, value_weight, w_out, pack_small(w_router, norm_attn, norm_moe))
    packed, cot_own, cot_col, query, keys, values, attended, hidden_one, normed_two, gates, normed_one = front(
        tokens, prefix, routes.T, packed_own, cotangent, cosine, sine, experts, kv_width, spread
    )
    x_own, x_col, gates_own, gates_col, back, d_gates, mixture, cot_oth = moe_own(
        normed_two, gates, cot_own, cot_col, w_gate, w_up, w_down, spread
    )
    mixture = lax.psum_scatter(mixture.reshape(-1, width), "shard", scatter_dimension=0, tiled=True)
    d_tokens, shares = attention_back(
        prefix, tokens, cotangent, cosine, sine, packed, query, keys, values, attended, normed_one, normed_two, hidden_one,
        gates, d_gates.reshape(experts, count), back,
    )
    shares = shares.reshape(width, -1)
    if spread:
        x_own, shares = lax.optimization_barrier((x_own, shares))
        x_oth, cot_oth, gates_oth, sums = moe_spread_sums(
            x_own, cot_own, x_col, cot_col, cot_oth, gates_own, gates_col, w_gate, w_up, w_down
        )
        shares = lax.psum_scatter(shares, "shard", scatter_dimension=0, tiled=True)
        shares, gates_oth = lax.optimization_barrier((shares, gates_oth))
        sums = moe_sums(x_oth, cot_oth, gates_oth, w_gate, w_up, w_down, sums)
    else:
        sums = moe_sums(x_own, cot_own, gates_own, w_gate, w_up, w_down)
        sums = [lax.psum(a.astype(bf16), "rep").astype(f32) for a in sums]
        shares = lax.psum_scatter(shares, "shard", scatter_dimension=0, tiled=True)
    d_w_gate, d_w_up, d_w_down = sums
    totals = lax.psum(shares, "rep").astype(f32)
    cuts = [width, width + kv_width, width + 2 * kv_width, 2 * width + 2 * kv_width]
    d_wq, d_wk, d_wv, d_wo, small = jnp.split(totals, cuts, axis=1)
    result = (hidden_one + mixture.astype(f32)).astype(bf16)
    return (
        result, d_tokens, d_wq, d_wk, d_wv, d_wo, small[:, experts], small[:, experts + 1],
        small[:, :experts], d_w_gate, d_w_up, d_w_down,
    )


def solution(mesh):
    rows = P(("rep", "shard"), None)
    one, two, three = P("shard"), P("shard", None), P("shard", None, None)
    return jax.shard_map(
        body,
        mesh=mesh,
        in_specs=(rows, P(("rep", "shard")), rows, rows, two, two, two, two, one, one, two, three, three, three),
        out_specs=(rows, rows, two, two, two, two, one, one, two, three, three, three),
        check_vma=False,
    )
```

profile of v0, /device:TPU:0, one launch (start us, length us, event | category | flops | bytes accessed | tf_op | source)
XLA Modules:
  0.0 398.4 jit_solution(16256275797822182412)
XLA Ops:
  7.2 0.0 reduce-scatter.5.cloned.1.call-start
  7.9 0.7 pad_maximum_fusion
  8.6 0.1 copy.37
  8.7 0.6 pad.4.ws_hbm
  9.4 64.9 %front.1 = (bf16[8,128,3200]{2,1,0:T(8,128)(2,1)}, bf16[8,256,1024]{2,1,0:T(8,128)(2,1)}, bf16[4,256,1024]{2,1,0:T(8,128)(2,1)}, bf16[256,1024]{1,0:T(8,128)(2,1...) custom-call(s32[1]{0:T(128)S(6)} %copy.47.prefix_ref, ...), custom_call_target="tpu_custom_call" | custom-call | tf_op jit(solution)/shard_map/front/pallas_call | solution.py:507
  74.3 86.0 %own_experts.1 = (bf16[8,256,1024]{2,1,0:T(8,128)(2,1)}, bf16[4,256,1024]{2,1,0:T(8,128)(2,1)}, f32[8,32,256]{2,1,0:T(8,128)}, f32[4,32,256]{2,1,0:T(8,128)}, f3...) custom-call(bf16[256,1024]{1,0:T(8,128)(2,1)} %get-tuple-element.47., ...), custom_call_target="tpu_custom_call" | custom-call | tf_op jit(solution)/shard_map/own_experts/pallas_call | solution.py:765
  160.3 0.0 reduce-scatter.5.cloned.1.call-update
  160.3 0.0 reduce-scatter.7.cloned.1.call-start
  160.3 1.4 reshape.34.dg_ref
  161.7 24.9 %attention_back.1 = (f32[256,1024]{1,0:T(8,128)}, bf16[8,128,3200]{2,1,0:T(8,128)(2,1)}) custom-call(s32[1]{0:T(128)S(6)} %copy.47.prefix_ref, bf16[256,1024]{1,0:T(8,128)(2,1)} %tok_ref.3, bf16[256,1024]{1,0:T(8,128)(2,1)} %cot_ref.3, f32[256,128]{1,0:T(8,128)} %constant.7.clone.cos_ref, f32[256,128]{1,0:T(8,128)} %constant.8.clone.sin_ref, ...), custom_call_target="tpu_custom_call" | custom-call | tf_op jit(solution)/shard_map/attention_back/pallas_call | solution.py:876
  186.6 0.0 reduce-scatter.7.cloned.1.call-update
  186.6 0.0 all-reduce.3.cloned.1.call-start
  186.7 0.0 copy-start.1
  186.7 145.3 %spread_expert_sums.1 = (bf16[3,8,256,1024]{3,2,1,0:T(8,128)(2,1)}, bf16[3,8,256,1024]{3,2,1,0:T(8,128)(2,1)}, f32[4,1024,512]{2,1,0:T(8,128)}, f32[4,1024,512]{...) custom-call(bf16[8,256,1024]{2,1,0:T(8,128)(2,1)} %get-tuple-element.64.xown_hbm, ...), custom_call_target="tpu_custom_call", output_to_operand_aliasing={{1}: (9, {})} | custom-call | flops 77309411328 | bytes 33554432 | tf_op jit(solution)/shard_map/spread_expert_sums/pallas_call | solution.py:1026
  332.0 0.0 reduce-scatter.5.cloned.1.call-done
  332.0 0.0 copy-done.1
  332.0 2.0 add_convert_fusion
  334.0 0.0 reduce-scatter.7.cloned.1.call-done
  334.0 2.2 copy.44
  336.2 0.0 all-reduce.3.cloned.1.call-update
  336.2 48.3 %expert_sums.1 = (f32[4,1024,512]{2,1,0:T(8,128)}, f32[4,1024,512]{2,1,0:T(8,128)}, f32[4,512,1024]{2,1,0:T(8,128)}) custom-call(bf16[3,8,256,1024]{3,2,1,0:T(8,128)(2,1)} %get-tuple-element.71.x_hbm, bf16[3,8,256,1024]{3,2,1,0:T(8,128)(2,1)} %get-tuple-element.72.c_hbm, f32[8,32,256]{2,1,0:T(8,128)} %get-tuple-element.73.g_ref, ...), custom_call_target="tpu_custom_call" | custom-call | flops 19327352832 | bytes 58720256 | tf_op jit(solution)/shard_map/expert_sums/pallas_call | solution.py:158
  384.5 0.0 all-reduce.3.cloned.1.call-done
  384.5 0.0 copy-start
  384.5 1.1 fusion.1
  385.6 0.8 copy.41
  386.5 0.8 copy.40
  387.3 1.1 fusion
  388.4 1.0 copy.42
  389.4 1.0 copy.39
  390.4 0.0 copy-done
  390.4 0.1 convert_element_type.13
  390.5 0.5 slice_bitcast_fusion
  391.0 0.6 slice.17
Async XLA Ops:
  7.2 324.8 %reduce-scatter.5.cloned.1.call-start = ((), (), s32[]{:S(2)}) async-start(), calls=%async_computation.2 | async-start | bytes 4718592 | tf_op jit(solution)/shard_map/reduce_scatter | solution.py:1081
  160.3 173.7 %reduce-scatter.7.cloned.1.call-start = ((), (), s32[]{:S(2)}) async-start(), calls=%async_computation.4 | async-start | bytes 7372800
  186.6 197.9 %all-reduce.3.cloned.1.call-start = ((), (), s32[]{:S(2)}) async-start(), calls=%async_computation.3 | async-start | bytes 1638400 | tf_op jit(solution)/shard_map/psum | solution.py:1100
  186.7 145.3 %copy-start.1 = (f32[256,1024]{1,0:T(8,128)S(1)}, f32[256,1024]{1,0:T(8,128)}, u32[]{:S(2)}) copy-start(f32[256,1024]{1,0:T(8,128)} %get-tuple-element.46.hid_ref) | copy-start | bytes 3145732
  384.5 5.9 %copy-start = (bf16[128,3200]{0,1:T(8,128)(2,1)S(1)}, bf16[128,3200]{0,1:T(8,128)(2,1)}, u32[]{:S(2)}) copy-start(bf16[128,3200]{0,1:T(8,128)(2,1)} %all-reduce.3.cloned.1.call-done) | copy-start | bytes 2457604
Sparse Core Ops, SparseCore 0:
  160.4 57.3 reduce-scatter.4
  222.2 75.2 reduce-scatter.6
  336.3 42.0 all-reduce.2
where the time goes:
time: 403 us; the launch traced here: 398 us
  Pallas kernels  369 us (92%)
  between operations  14.7 us (4%)
  local copies, waits for them, and re-layouts  11.3 us (3%)
    pallas_call x1, Pallas kernels, moe_spread_sums(): pl.pallas_call(functools.partial(spread_kernel, nb), out_shape=[jax.Shape...  145 us
    pallas_call x1, Pallas kernels, moe_own(): pl.pallas_call(functools.partial(own_kernel, spread, nb), out_shape=[sds(...  86 us
    pallas_call x1, Pallas kernels, front(): pl.pallas_call(functools.partial(front_kernel, spread), out_shape=[sds((s...  64.9 us
    pallas_call x1, Pallas kernels, moe_sums(): pl.pallas_call(functools.partial(sums_kernel, nb, bool(starts)), out_shap...  48.3 us
    pallas_call x1, Pallas kernels, attention_back(): pl.pallas_call(back_kernel, out_shape=[sds((count, width), f32), sds(pack...  24.9 us
  transfers between devices with their start and end apart: 3, of which 0 were waited for; matrix products, arithmetic and copies ran while one was open for 1% of the time, Pallas kernels for 55%

commit v1 on v0

--- a/solution.py
+++ b/solution.py
@@ -435,8 +435,8 @@
     scaled = inputs * norm_scale(inputs)
     for step in range(gather.steps):
         gather.forward(step)
+    near.start()
     gather.finish()
-    near.start()
     keep = pltpu.make_async_copy(wbuf, wall_out, lsem.at[1])
     keep.start()
     cut = [0, width, width + kv_width, width + 2 * kv_width, 2 * width + 2 * kv_width]
@@ -459,7 +459,6 @@
     v_out[...] = qkv_ref[:, cut[2]:cut[3]].astype(bf16)
     prefix_len = prefix_ref[0]
 
-    near.forward(0)
 
     def head(j, carry):
         keys = one_head_twice(k_out[:, lanes(j // 2)], j % 2)
@@ -468,6 +467,10 @@
         both = dot(prob.astype(bf16), values)
         low = lax.broadcasted_iota(jnp.int32, (count, LANES), 1) < HEAD_SIZE
         att_out[:, lanes(j)] = jnp.where(low, both[:count], both[count:]).astype(bf16)
+
+        @pl.when(j == 2)
+        def _():
+            near.forward(0)
         return carry
     lax.fori_loop(0, KEY_VALUE_HEADS, head, 0)
     for step in range(1, near.steps):
@@ -887,7 +890,7 @@
 
 def spread_kernel(nb, xown_hbm, cown_hbm, xcol_hbm, ccol_hbm, gown_ref, gcol_ref, wg_hbm, wu_hbm, wd_hbm, coth_in,
                   xoth_hbm, coth_hbm, og_hbm, ou_hbm, od_hbm, glast_ref,
-                  xbuf, cbuf, wg, wu, wd, ag, au, ad, xg_ref, cg_ref, sg_ref, goth, send, recv, bsem, wsem, *sems):
+                  xbuf, cbuf, wg, wu, wd, ag, au, ad, xg_ref, cg_ref, sg_ref, goth, send, recv, bsem, wsem, osem, *sems):
     xsems, csems = sems[:7], sems[7:]
     local = wg.shape[0]
     shards = gown_ref.shape[0]
@@ -911,7 +914,10 @@
         return (pltpu.make_async_copy(x.at[pl.ds(q * nb, nb)], xbuf.at[slot], bsem.at[0, slot]),
                 pltpu.make_async_copy(c.at[pl.ds(q * nb, nb)], cbuf.at[slot], bsem.at[1, slot]))
 
-    def replica(x, c, g, midway, last):
+    def out_copies(l):
+        return [pltpu.make_async_copy(a.at[l], b.at[l], osem.at[i, l]) for i, (a, b) in enumerate(((ag, og_hbm), (au, ou_hbm), (ad, od_hbm)))]
+
+    def replica(x, c, g, midway, last, final=False):
         for copy in fetch(x, c, 0, 0):
             copy.start()
 
@@ -937,6 +943,12 @@
                 @pl.when((q == chunks // 2) & (l == 0))
                 def _():
                     midway()
+
+                if final:
+                    @pl.when(q == chunks - 1)
+                    def _():
+                        for copy in out_copies(l):
+                            copy.start()
                 return carry
             lax.fori_loop(0, local, expert, 0)
             return carry
@@ -1004,14 +1016,12 @@
     replica(xown_hbm, cown_hbm, gown_ref, midway_own, last_own)
     replica(xoth_hbm.at[1], coth_hbm.at[1], goth.at[1], midway_two, last_two)
     third, left = late_places(rep, reps)
-    replica(xoth_hbm.at[third], coth_hbm.at[third], goth.at[third], midway_three, last_three)
+    replica(xoth_hbm.at[third], coth_hbm.at[third], goth.at[third], midway_three, last_three, True)
     xs.sent_straight()
     glast_ref[...] = goth[left]
-    outs = [pltpu.make_async_copy(a, b, wsem.at[i]) for i, (a, b) in enumerate(((ag, og_hbm), (au, ou_hbm), (ad, od_hbm)))]
-    for copy in outs:
-        copy.start()
-    for copy in outs:
-        copy.wait()
+    for l in range(local):
+        for copy in out_copies(l):
+            copy.wait()
 
 
 def moe_spread_sums(xown, cown, xcol, ccol, coth, gown, gcol, wg, wu, wd, nb=4):
@@ -1037,7 +1047,7 @@
             pltpu.VMEM((local, rows, width), bf16), pltpu.VMEM((local, rows, width), bf16), pltpu.VMEM((local, rows, 1), f32),
             pltpu.VMEM((reps - 1, shards, *gown.shape[1:]), f32),
             pltpu.SemaphoreType.DMA((reps - 1, n)), pltpu.SemaphoreType.DMA((reps - 1, n)),
-            pltpu.SemaphoreType.DMA((2, 2)), pltpu.SemaphoreType.DMA((3,)),
+            pltpu.SemaphoreType.DMA((2, 2)), pltpu.SemaphoreType.DMA((3,)), pltpu.SemaphoreType.DMA((3, local)),
             *Spread.semaphores(shards, reps), *Spread.semaphores(shards, reps),
         ],
         compiler_params=pltpu.CompilerParams(vmem_limit_bytes=60 << 20, has_side_effects=True, collective_id=3),

time: 403 us -> 392 us (0.973)
  Pallas kernels: 369 us -> 358 us
    pallas_call x1, Pallas kernels: 145 us -> 137 us  [moe_spread_sums(): pl.pallas_call(functools.partial(spread_kernel, nb), out_shape=[jax.Shape...]
  transfers between devices with their start and end apart: 3 -> 3, of which waited for: 0 -> 0; matrix products, arithmetic and copies ran while one was open for 1% -> 1% of each run, Pallas kernels for 55% -> 54%
where the time goes in v1:
time: 392 us; the launch traced here: 387 us
  Pallas kernels  358 us (91%)
  between operations  14.7 us (4%)
  local copies, waits for them, and re-layouts  11.3 us (3%)
    pallas_call x1, Pallas kernels, moe_spread_sums(): pl.pallas_call(functools.partial(spread_kernel, nb), out_shape=[jax.Shape...  137 us
    pallas_call x1, Pallas kernels, moe_own(): pl.pallas_call(functools.partial(own_kernel, spread, nb), out_shape=[sds(...  86.6 us
    pallas_call x1, Pallas kernels, front(): pl.pallas_call(functools.partial(front_kernel, spread), out_shape=[sds((s...  61.2 us
    pallas_call x1, Pallas kernels, moe_sums(): pl.pallas_call(functools.partial(sums_kernel, nb, bool(starts)), out_shap...  48.3 us
    pallas_call x1, Pallas kernels, attention_back(): pl.pallas_call(back_kernel, out_shape=[sds((count, width), f32), sds(pack...  24.8 us
  transfers between devices with their start and end apart: 3, of which 0 were waited for; matrix products, arithmetic and copies ran while one was open for 1% of the time, Pallas kernels for 54%

profile of v1, /device:TPU:0, one launch (start us, length us, event | category | flops | bytes accessed | tf_op | source)
XLA Modules:
  0.0 387.4 jit_solution(3153733525965032127)
XLA Ops:
  7.2 0.0 reduce-scatter.5.cloned.1.call-start
  7.9 0.7 pad_maximum_fusion
  8.6 0.1 copy.37
  8.7 0.6 pad.4.ws_hbm
  9.4 61.2 %front.1 = (bf16[8,128,3200]{2,1,0:T(8,128)(2,1)}, bf16[8,256,1024]{2,1,0:T(8,128)(2,1)}, bf16[4,256,1024]{2,1,0:T(8,128)(2,1)}, bf16[256,1024]{1,0:T(8,128)(2,1...) custom-call(s32[1]{0:T(128)S(6)} %copy.47.prefix_ref, ...), custom_call_target="tpu_custom_call" | custom-call | tf_op jit(solution)/shard_map/front/pallas_call | solution.py:510
  70.5 86.6 %own_experts.1 = (bf16[8,256,1024]{2,1,0:T(8,128)(2,1)}, bf16[4,256,1024]{2,1,0:T(8,128)(2,1)}, f32[8,32,256]{2,1,0:T(8,128)}, f32[4,32,256]{2,1,0:T(8,128)}, f3...) custom-call(bf16[256,1024]{1,0:T(8,128)(2,1)} %get-tuple-element.47., ...), custom_call_target="tpu_custom_call" | custom-call | tf_op jit(solution)/shard_map/own_experts/pallas_call | solution.py:768
  157.2 0.0 reduce-scatter.5.cloned.1.call-update
  157.2 0.0 reduce-scatter.7.cloned.1.call-start
  157.3 1.4 reshape.34.dg_ref
  158.7 24.8 %attention_back.1 = (f32[256,1024]{1,0:T(8,128)}, bf16[8,128,3200]{2,1,0:T(8,128)(2,1)}) custom-call(s32[1]{0:T(128)S(6)} %copy.47.prefix_ref, bf16[256,1024]{1,0:T(8,128)(2,1)} %tok_ref.3, bf16[256,1024]{1,0:T(8,128)(2,1)} %cot_ref.3, f32[256,128]{1,0:T(8,128)} %constant.7.clone.cos_ref, f32[256,128]{1,0:T(8,128)} %constant.8.clone.sin_ref, ...), custom_call_target="tpu_custom_call" | custom-call | tf_op jit(solution)/shard_map/attention_back/pallas_call | solution.py:879
  183.5 0.0 reduce-scatter.7.cloned.1.call-update
  183.5 0.0 all-reduce.3.cloned.1.call-start
  183.6 0.0 copy-start.1
  183.6 137.3 %spread_expert_sums.1 = (bf16[3,8,256,1024]{3,2,1,0:T(8,128)(2,1)}, bf16[3,8,256,1024]{3,2,1,0:T(8,128)(2,1)}, f32[4,1024,512]{2,1,0:T(8,128)}, f32[4,1024,512]{...) custom-call(bf16[8,256,1024]{2,1,0:T(8,128)(2,1)} %get-tuple-element.64.xown_hbm, ...), custom_call_target="tpu_custom_call", output_to_operand_aliasing={{1}: (9, {})} | custom-call | flops 77309411328 | bytes 33554432 | tf_op jit(solution)/shard_map/spread_expert_sums/pallas_call | solution.py:1036
  320.9 0.0 reduce-scatter.5.cloned.1.call-done
  321.0 0.0 copy-done.1
  321.0 2.0 add_convert_fusion
  323.0 0.0 reduce-scatter.7.cloned.1.call-done
  323.0 2.2 copy.44
  325.2 0.0 all-reduce.3.cloned.1.call-update
  325.2 48.3 %expert_sums.1 = (f32[4,1024,512]{2,1,0:T(8,128)}, f32[4,1024,512]{2,1,0:T(8,128)}, f32[4,512,1024]{2,1,0:T(8,128)}) custom-call(bf16[3,8,256,1024]{3,2,1,0:T(8,128)(2,1)} %get-tuple-element.71.x_hbm, bf16[3,8,256,1024]{3,2,1,0:T(8,128)(2,1)} %get-tuple-element.72.c_hbm, f32[8,32,256]{2,1,0:T(8,128)} %get-tuple-element.73.g_ref, ...), custom_call_target="tpu_custom_call" | custom-call | flops 19327352832 | bytes 58720256 | tf_op jit(solution)/shard_map/expert_sums/pallas_call | solution.py:158
  373.5 0.0 all-reduce.3.cloned.1.call-done
  373.5 0.0 copy-start
  373.5 1.1 fusion.1
  374.6 0.8 copy.41
  375.4 0.8 copy.40
  376.3 1.1 fusion
  377.4 1.0 copy.42
  378.4 1.0 copy.39
  379.4 0.0 copy-done
  379.4 0.1 convert_element_type.13
  379.5 0.5 slice_bitcast_fusion
  380.0 0.6 slice.17
Async XLA Ops:
  7.2 313.8 %reduce-scatter.5.cloned.1.call-start = ((), (), s32[]{:S(2)}) async-start(), calls=%async_computation.2 | async-start | bytes 4718592 | tf_op jit(solution)/shard_map/reduce_scatter | solution.py:1091
  157.2 165.7 %reduce-scatter.7.cloned.1.call-start = ((), (), s32[]{:S(2)}) async-start(), calls=%async_computation.4 | async-start | bytes 7372800
  183.5 190.0 %all-reduce.3.cloned.1.call-start = ((), (), s32[]{:S(2)}) async-start(), calls=%async_computation.3 | async-start | bytes 1638400 | tf_op jit(solution)/shard_map/psum | solution.py:1110
  183.6 137.4 %copy-start.1 = (f32[256,1024]{1,0:T(8,128)S(1)}, f32[256,1024]{1,0:T(8,128)}, u32[]{:S(2)}) copy-start(f32[256,1024]{1,0:T(8,128)} %get-tuple-element.46.hid_ref) | copy-start | bytes 3145732
  373.5 5.9 %copy-start = (bf16[128,3200]{0,1:T(8,128)(2,1)S(1)}, bf16[128,3200]{0,1:T(8,128)(2,1)}, u32[]{:S(2)}) copy-start(bf16[128,3200]{0,1:T(8,128)(2,1)} %all-reduce.3.cloned.1.call-done) | copy-start | bytes 2457604
Sparse Core Ops, SparseCore 0:
  157.4 57.2 reduce-scatter.4
  219.1 75.5 reduce-scatter.6
  325.3 41.9 all-reduce.2

commit v2 on v1

--- a/solution.py
+++ b/solution.py
@@ -114,8 +114,6 @@
         ag[...] = jnp.zeros_like(ag)
         au[...] = jnp.zeros_like(au)
         ad[...] = jnp.zeros_like(ad)
-    for cp in weights:
-        cp.wait()
 
     def chunk(i, carry):
         slot = lax.rem(i, 2)
@@ -130,6 +128,12 @@
                          pl.multiple_of(b * CAP, CAP))
             return carry
         lax.fori_loop(0, nb, block, 0)
+
+        @pl.when(i == 0)
+        def _():
+            for cp in weights:
+                cp.wait()
+
         def expert(l, carry):
             if starts:
                 @pl.when(i == 0)
@@ -917,7 +921,7 @@
     def out_copies(l):
         return [pltpu.make_async_copy(a.at[l], b.at[l], osem.at[i, l]) for i, (a, b) in enumerate(((ag, og_hbm), (au, ou_hbm), (ad, od_hbm)))]
 
-    def replica(x, c, g, midway, last, final=False):
+    def replica(x, c, g, midway, last, opening=False, final=False):
         for copy in fetch(x, c, 0, 0):
             copy.start()
 
@@ -936,6 +940,11 @@
                              pl.multiple_of(b * CAP, CAP))
                 return carry
             lax.fori_loop(0, nb, block, 0)
+            if opening:
+                @pl.when(q == 0)
+                def _():
+                    for copy in weights:
+                        copy.wait()
 
             def expert(l, carry):
                 add_expert(l, xg_ref, cg_ref, sg_ref, wg, wu, wd, ag, au, ad)
@@ -970,8 +979,6 @@
     ag[...] = jnp.zeros_like(ag)
     au[...] = jnp.zeros_like(au)
     ad[...] = jnp.zeros_like(ad)
-    for copy in weights:
-        copy.wait()
 
     def midway_own():
         xs.forward(2)
@@ -1013,10 +1020,10 @@
         on_ends(lambda: each(Spread.end, reps - 1), lambda: each(Spread.end, 1))
         pl.when(rep > 0)(lambda: xs.end_across(0))
 
-    replica(xown_hbm, cown_hbm, gown_ref, midway_own, last_own)
+    replica(xown_hbm, cown_hbm, gown_ref, midway_own, last_own, opening=True)
     replica(xoth_hbm.at[1], coth_hbm.at[1], goth.at[1], midway_two, last_two)
     third, left = late_places(rep, reps)
-    replica(xoth_hbm.at[third], coth_hbm.at[third], goth.at[third], midway_three, last_three, True)
+    replica(xoth_hbm.at[third], coth_hbm.at[third], goth.at[third], midway_three, last_three, final=True)
     xs.sent_straight()
     glast_ref[...] = goth[left]
     for l in range(local):

time: 392 us -> 390 us (level)
  Pallas kernels: 358 us -> 354 us
    pallas_call x1, Pallas kernels: 137 us -> 133 us  [moe_spread_sums(): pl.pallas_call(functools.partial(spread_kernel, nb), out_shape=[jax.Shape...]
where the time goes in v2:
time: 390 us; the launch traced here: 383 us
  Pallas kernels  354 us (91%)
  between operations  14.7 us (4%)
  local copies, waits for them, and re-layouts  11.3 us (3%)
    pallas_call x1, Pallas kernels, moe_spread_sums(): pl.pallas_call(functools.partial(spread_kernel, nb), out_shape=[jax.Shape...  133 us
    pallas_call x1, Pallas kernels, moe_own(): pl.pallas_call(functools.partial(own_kernel, spread, nb), out_shape=[sds(...  86.6 us
    pallas_call x1, Pallas kernels, front(): pl.pallas_call(functools.partial(front_kernel, spread), out_shape=[sds((s...  61.2 us
    pallas_call x1, Pallas kernels, moe_sums(): pl.pallas_call(functools.partial(sums_kernel, nb, bool(starts)), out_shap...  48.3 us
    pallas_call x1, Pallas kernels, attention_back(): pl.pallas_call(back_kernel, out_shape=[sds((count, width), f32), sds(pack...  24.8 us
  transfers between devices with their start and end apart: 3, of which 0 were waited for; matrix products, arithmetic and copies ran while one was open for 1% of the time, Pallas kernels for 54%

profile of v2, /device:TPU:0, one launch (start us, length us, event | category | flops | bytes accessed | tf_op | source)
XLA Modules:
  0.0 383.4 jit_solution(12334702978488401894)
XLA Ops:
  7.2 0.0 reduce-scatter.5.cloned.1.call-start
  7.9 0.7 pad_maximum_fusion
  8.6 0.1 copy.37
  8.7 0.6 pad.4.ws_hbm
  9.4 61.2 %front.1 = (bf16[8,128,3200]{2,1,0:T(8,128)(2,1)}, bf16[8,256,1024]{2,1,0:T(8,128)(2,1)}, bf16[4,256,1024]{2,1,0:T(8,128)(2,1)}, bf16[256,1024]{1,0:T(8,128)(2,1...) custom-call(s32[1]{0:T(128)S(6)} %copy.47.prefix_ref, ...), custom_call_target="tpu_custom_call" | custom-call | tf_op jit(solution)/shard_map/front/pallas_call | solution.py:514
  70.5 86.6 %own_experts.1 = (bf16[8,256,1024]{2,1,0:T(8,128)(2,1)}, bf16[4,256,1024]{2,1,0:T(8,128)(2,1)}, f32[8,32,256]{2,1,0:T(8,128)}, f32[4,32,256]{2,1,0:T(8,128)}, f3...) custom-call(bf16[256,1024]{1,0:T(8,128)(2,1)} %get-tuple-element.47., ...), custom_call_target="tpu_custom_call" | custom-call | tf_op jit(solution)/shard_map/own_experts/pallas_call | solution.py:772
  157.2 0.0 reduce-scatter.5.cloned.1.call-update
  157.2 0.0 reduce-scatter.7.cloned.1.call-start
  157.3 1.4 reshape.34.dg_ref
  158.7 24.8 %attention_back.1 = (f32[256,1024]{1,0:T(8,128)}, bf16[8,128,3200]{2,1,0:T(8,128)(2,1)}) custom-call(s32[1]{0:T(128)S(6)} %copy.47.prefix_ref, bf16[256,1024]{1,0:T(8,128)(2,1)} %tok_ref.3, bf16[256,1024]{1,0:T(8,128)(2,1)} %cot_ref.3, f32[256,128]{1,0:T(8,128)} %constant.7.clone.cos_ref, f32[256,128]{1,0:T(8,128)} %constant.8.clone.sin_ref, ...), custom_call_target="tpu_custom_call" | custom-call | tf_op jit(solution)/shard_map/attention_back/pallas_call | solution.py:883
  183.5 0.0 reduce-scatter.7.cloned.1.call-update
  183.5 0.0 all-reduce.3.cloned.1.call-start
  183.6 0.0 copy-start.1
  183.6 133.4 %spread_expert_sums.1 = (bf16[3,8,256,1024]{3,2,1,0:T(8,128)(2,1)}, bf16[3,8,256,1024]{3,2,1,0:T(8,128)(2,1)}, f32[4,1024,512]{2,1,0:T(8,128)}, f32[4,1024,512]{...) custom-call(bf16[8,256,1024]{2,1,0:T(8,128)(2,1)} %get-tuple-element.64.xown_hbm, ...), custom_call_target="tpu_custom_call", output_to_operand_aliasing={{1}: (9, {})} | custom-call | flops 77309411328 | bytes 33554432 | tf_op jit(solution)/shard_map/spread_expert_sums/pallas_call | solution.py:1043
  317.0 0.0 reduce-scatter.5.cloned.1.call-done
  317.0 0.0 copy-done.1
  317.0 2.0 add_convert_fusion
  319.0 0.0 reduce-scatter.7.cloned.1.call-done
  319.0 2.2 copy.44
  321.2 0.0 all-reduce.3.cloned.1.call-update
  321.2 48.3 %expert_sums.1 = (f32[4,1024,512]{2,1,0:T(8,128)}, f32[4,1024,512]{2,1,0:T(8,128)}, f32[4,512,1024]{2,1,0:T(8,128)}) custom-call(bf16[3,8,256,1024]{3,2,1,0:T(8,128)(2,1)} %get-tuple-element.71.x_hbm, bf16[3,8,256,1024]{3,2,1,0:T(8,128)(2,1)} %get-tuple-element.72.c_hbm, f32[8,32,256]{2,1,0:T(8,128)} %get-tuple-element.73.g_ref, ...), custom_call_target="tpu_custom_call" | custom-call | flops 19327352832 | bytes 58720256 | tf_op jit(solution)/shard_map/expert_sums/pallas_call | solution.py:162
  369.5 0.0 all-reduce.3.cloned.1.call-done
  369.5 0.0 copy-start
  369.5 1.1 fusion.1
  370.6 0.8 copy.41
  371.4 0.8 copy.40
  372.3 1.1 fusion
  373.4 1.0 copy.42
  374.4 1.0 copy.39
  375.4 0.0 copy-done
  375.4 0.1 convert_element_type.13
  375.5 0.5 slice_bitcast_fusion
  376.0 0.6 slice.17
Async XLA Ops:
  7.2 309.8 %reduce-scatter.5.cloned.1.call-start = ((), (), s32[]{:S(2)}) async-start(), calls=%async_computation.2 | async-start | bytes 4718592 | tf_op jit(solution)/shard_map/reduce_scatter | solution.py:1098
  157.2 161.8 %reduce-scatter.7.cloned.1.call-start = ((), (), s32[]{:S(2)}) async-start(), calls=%async_computation.4 | async-start | bytes 7372800
  183.5 186.0 %all-reduce.3.cloned.1.call-start = ((), (), s32[]{:S(2)}) async-start(), calls=%async_computation.3 | async-start | bytes 1638400 | tf_op jit(solution)/shard_map/psum | solution.py:1117
  183.6 133.4 %copy-start.1 = (f32[256,1024]{1,0:T(8,128)S(1)}, f32[256,1024]{1,0:T(8,128)}, u32[]{:S(2)}) copy-start(f32[256,1024]{1,0:T(8,128)} %get-tuple-element.46.hid_ref) | copy-start | bytes 3145732
  369.5 5.9 %copy-start = (bf16[128,3200]{0,1:T(8,128)(2,1)S(1)}, bf16[128,3200]{0,1:T(8,128)(2,1)}, u32[]{:S(2)}) copy-start(bf16[128,3200]{0,1:T(8,128)(2,1)} %all-reduce.3.cloned.1.call-done) | copy-start | bytes 2457604
Sparse Core Ops, SparseCore 0:
  157.4 57.2 reduce-scatter.4
  219.1 72.6 reduce-scatter.6
  321.3 43.0 all-reduce.2
